TPU v7x, 256 devices: a whole 4x4x8 slice. The times are simulated.
256 devices in a mesh: gx: 32 (over y, z), gy: 8 (over x, core).
Axes of the slice: x: 4, y: 4, z: 8, core: 2. Of those that a mesh axis runs over, the one named last changes fastest.
Arguments:
- normed: bfloat16 [163840, 1024], P(('gx', 'gy')), may hold values from -6 to 6
- grad_query: bfloat16 [163840, 1024], P(('gx', 'gy')), may hold values from -0.25 to 0.25
- grad_key: bfloat16 [163840, 1024], P(('gx', 'gy')), may hold values from -0.25 to 0.25
- error: bfloat16 [512, 1024, 1024], P(('gx', 'gy')), may hold values from -8 to 8
- start_factor: float32 [2, 32, 1024], replicated, may hold values from -6 to 6
Outputs:
- new_error: bfloat16 [512, 1024, 1024], P(('gx', 'gy'))
- left_factor: float32 [2, 32, 1024], replicated
- right_factor: float32 [2, 32, 1024], replicated
All inputs are finite; a program needn't handle non-finite values.
Results may differ from a plain program's by a relative error of at most 0.001.
Values sent between devices are 32-bit elements; how exact they have to be, the bound alone decides.
A program may use at most 64 MiB of HBM per device.

v0:
```python
import jax
import jax.numpy as jnp
from jax import lax
from jax.sharding import PartitionSpec as P

HIGHEST = lax.Precision.HIGHEST
CONTRACT = (((0,), (0,)), ((), ()))


def gram_of(factor_rows):
    return jnp.einsum("bki,bli->bkl", factor_rows, factor_rows, precision=HIGHEST)


def solve_rows(gram_matrix, factor_rows):
    width = gram_matrix.shape[-1]
    identity = jnp.eye(width, dtype=jnp.float32)
    trace_value = jnp.trace(gram_matrix, axis1=1, axis2=2)
    shift_value = 1e-06 * (trace_value / width + 1.0)
    lower_factor = jnp.linalg.cholesky(gram_matrix + shift_value[:, None, None] * identity)
    return lax.linalg.triangular_solve(lower_factor, factor_rows, left_side=True, lower=True)


def local_left(merged, start_rows):
    return jnp.einsum("bkj,bij->bki", start_rows, merged, precision=HIGHEST)


def local_right(left_rows, merged):
    return jnp.einsum("bki,bij->bkj", left_rows, merged, precision=HIGHEST)


def single_factors(merged, start_rows, replicas):
    left_total = lax.psum(local_left(merged, start_rows), ("gx", "gy"))
    left_rows = solve_rows(gram_of(left_total), left_total)
    right_total = lax.psum(local_right(left_rows, merged), ("gx", "gy"))
    return (left_rows, right_total / replicas)


def on_device(normed, grad_query, grad_key, error, start_factor):
    replicas = lax.axis_size("gx") * lax.axis_size("gy")
    query_grad = lax.dot_general(normed, grad_query, CONTRACT, preferred_element_type=jnp.float32)
    query_merged = query_grad + error[0].astype(jnp.float32)
    query_left, query_right = single_factors(query_merged[None], start_factor[0:1], replicas)
    key_grad = lax.dot_general(normed, grad_key, CONTRACT, preferred_element_type=jnp.float32)
    key_merged = key_grad + error[1].astype(jnp.float32)
    key_left, key_right = single_factors(key_merged[None], start_factor[1:2], replicas)
    merged = jnp.stack([query_merged, key_merged])
    left_rows = jnp.concatenate([query_left, key_left], axis=0)
    right_rows = jnp.concatenate([query_right, key_right], axis=0)
    approx = jnp.einsum("bki,bkj->bij", left_rows, right_rows, precision=HIGHEST)
    return ((merged - approx).astype(jnp.bfloat16), left_rows, right_rows)


def solution(mesh):
    placed = (
        P(("gx", "gy"), None),
        P(("gx", "gy"), None),
        P(("gx", "gy"), None),
        P(("gx", "gy"), None, None),
        P(),
    )
    return jax.shard_map(
        on_device,
        mesh=mesh,
        in_specs=placed,
        out_specs=(P(("gx", "gy"), None, None), P(), P()),
        check_vma=False,
    )
```

profile of v0, /device:TPU:2, one launch (start us, length us, event | category | flops | bytes accessed | tf_op | source)
XLA Modules:
  0.0 575.3 jit_solution(298892361489647621)
XLA Ops:
  7.2 0.0 copy-start
  7.2 0.0 copy-start.8
  7.2 0.0 all-reduce.7.cloned.1.call-start
  7.2 1.3 copy-done
  8.5 0.0 copy-start.7
  8.5 4.0 convert_add_fusion.1
  12.5 0.0 copy-done.8
  12.5 0.0 copy-done.7
  12.5 0.0 copy-start.1
  12.5 0.0 copy-start.6
  12.5 1.8 convert_add_fusion
  14.4 0.1 copy-done.1
  14.5 0.0 copy-done.6
  14.5 0.0 copy-start.2
  14.5 4.6 convolution_bitcast_fusion.3
  19.1 0.0 copy-done.2
  19.1 4.6 convolution_bitcast_fusion.2
  23.6 0.0 all-reduce.7.cloned.1.call-update
  23.7 0.2 all-reduce.5.cloned.1.call-start
  23.9 253.5 %all-reduce.7.cloned.1.call-done = (f32[1,32,1024]{2,1,0:T(8,128)}, f32[1,32,1024]{2,1,0:T(8,128)}) async-done(((f32[1,32,1024]{2,1,0:T(8,128)}, f32[1,32,1024]{2,1,0:T(8,128)}), (f32[1,32,1024]{2,1,0:T(8,128)}, f32[1,32,1024]{2,1,0:T(8,128)})) %all-reduce.7.cloned.1.call-update) | async-done | bytes 262160 | tf_op jit(solution)/shard_map/psum | solution.py:32
  277.4 1.8 select_reduce_fusion.2
  279.9 0.1 copy.13
  280.0 2.9 custom-call.10
  282.9 0.6 compare_reduce_fusion
  283.6 0.7 fusion.14
  284.2 2.4 custom-call.11
  286.7 1.2 fusion.1
  287.9 1.8 select_reduce_fusion.3
  290.4 0.1 copy.10
  290.5 2.9 custom-call.8
  293.5 0.6 compare_reduce_fusion.1
  294.1 0.7 fusion.13
  294.8 2.4 custom-call.9
  297.2 0.0 copy-start.3
  297.2 1.4 fusion.6
  298.6 5.3 convolution_bitcast_fusion.1
  304.0 0.0 copy-done.3
  304.0 3.1 convolution_bitcast_fusion
  307.1 0.0 all-reduce.5.cloned.1.call-update
  307.2 0.0 copy-start.4
  307.2 249.5 %all-reduce.5.cloned.1.call-done = (f32[1,32,1024]{2,1,0:T(8,128)}, f32[1,32,1024]{2,1,0:T(8,128)}) async-done(((f32[1,32,1024]{2,1,0:T(8,128)}, f32[1,32,1024]{2,1,0:T(8,128)}), (f32[1,32,1024]{2,1,0:T(8,128)}, f32[1,32,1024]{2,1,0:T(8,128)})) %all-reduce.5.cloned.1.call-update) | async-done | bytes 262160 | tf_op jit(solution)/shard_map/psum | solution.py:34
  556.7 1.0 broadcast_multiply_fusion
  557.7 0.0 copy-start.5
  557.7 10.7 %fusion = bf16[2,1024,1024]{2,1,0:T(8,128)(2,1)} fusion(f32[1,1024,1024]{2,1,0:T(8,128)} %bitcast.81, f32[1,1024,1024]{2,1,0:T(8,128)} %bitcast.80, f32[2,32,1024]{2,1,0:T(8,128)S(1)} %pad_maximum_fusion, f32[2,32,1024]{2,1,0:T(8,128)S(1)} %pad_maximum_fusion.1), kind=kOutput, calls=%fused_computation.1 | convolution fusion | flops 811597824 | bytes 13107200 | tf_op jit(solution)/shard_map/bki,bkj->bij/dot_general | solution.py:49
  568.4 0.0 copy-done.4
  568.4 0.0 copy-done.5
  (8 shorter events, 0.1 us)
Async XLA Ops:
  7.2 1.3 copy-start
  7.2 5.3 copy-start.8
  7.2 270.2 %all-reduce.7.cloned.1.call-start = ((), (), s32[]{:S(2)}) async-start(), calls=%async_computation.1 | async-start | bytes 524288 | tf_op jit(solution)/shard_map/psum | solution.py:32
  8.5 4.0 copy-start.7
  12.5 2.0 copy-start.1
  12.5 2.0 copy-start.6
  14.5 4.6 copy-start.2
  23.7 533.0 %all-reduce.5.cloned.1.call-start = ((), (), s32[]{:S(2)}) async-start(), calls=%async_computation | async-start | bytes 524288 | tf_op jit(solution)/shard_map/psum | solution.py:34
  297.2 6.7 %copy-start.3 = (f32[1024,1024]{1,0:T(8,128)S(1)}, f32[1024,1024]{1,0:T(8,128)}, u32[]{:S(2)}) copy-start(f32[1024,1024]{1,0:T(8,128)} %copy-done.2) | copy-start | bytes 12582916
  307.2 261.3 %copy-start.4 = (f32[2,32,1024]{2,1,0:T(8,128)}, f32[2,32,1024]{2,1,0:T(8,128)S(1)}, u32[]{:S(2)}) copy-start(f32[2,32,1024]{2,1,0:T(8,128)S(1)} %pad_maximum_fusion) | copy-start | bytes 786436
  557.7 10.7 %copy-start.5 = (f32[2,32,1024]{2,1,0:T(8,128)}, f32[2,32,1024]{2,1,0:T(8,128)S(1)}, u32[]{:S(2)}) copy-start(f32[2,32,1024]{2,1,0:T(8,128)S(1)} %pad_maximum_fusion.1) | copy-start | bytes 786436
Sparse Core Ops, SparseCore 0:
  23.8 253.5 all-reduce.6
  307.2 249.3 all-reduce.4
where the time goes:
time: 576 us; the launch traced here: 575 us
  waiting for transfers between devices  503 us (87%)
  matrix products  40.5 us (7%)
  between operations  15.5 us (3%)
  other arithmetic  14.4 us (2%)
    psum x1, waiting for transfers between devices, single_factors(): left_total = lax.psum(local_left(merged, start_rows), ('gx', 'gy'))  254 us
    psum x1, waiting for transfers between devices, single_factors(): right_total = lax.psum(local_right(left_rows, merged), ('gx', 'gy'))  250 us
  transfers between devices with their start and end apart: 2, of which 2 were waited for; matrix products, arithmetic and copies ran while one was open for 0% of the time, Pallas kernels for 0%

commit v1 on v0

--- a/solution.py
+++ b/solution.py
@@ -1,10 +1,19 @@
+import functools
 import jax
 import jax.numpy as jnp
 from jax import lax
 from jax.sharding import PartitionSpec as P
+from jax.lax import psum
 
 HIGHEST = lax.Precision.HIGHEST
 CONTRACT = (((0,), (0,)), ((), ()))
+
+
+def answer_chains(frame_in, which_axis, link_axis):
+    return psum(psum(frame_in, which_axis), link_axis)
+
+
+begin_targets_by_axis = functools.partial(answer_chains, which_axis="gy", link_axis="gx")
 
 
 def gram_of(factor_rows):
@@ -29,7 +38,7 @@
 
 
 def single_factors(merged, start_rows, replicas):
-    left_total = lax.psum(local_left(merged, start_rows), ("gx", "gy"))
+    left_total = begin_targets_by_axis(local_left(merged, start_rows))
     left_rows = solve_rows(gram_of(left_total), left_total)
     right_total = lax.psum(local_right(left_rows, merged), ("gx", "gy"))
     return (left_rows, right_total / replicas)

time: 576 us -> 535 us (0.929)
  waiting for transfers between devices: 503 us -> 463 us
    psum x1 -> x2, waiting for transfers between devices: 254 us -> 215 us  [answer_chains(): return psum(psum(frame_in, which_axis), link_axis)]
  transfers between devices with their start and end apart: 2 -> 3, of which waited for: 2 -> 3; matrix products, arithmetic and copies ran while one was open for 0% -> 0% of each run, Pallas kernels for 0% -> 0%
where the time goes in v1:
time: 535 us
  waiting for transfers between devices  463 us (87%)
  matrix products  40.5 us (8%)
  between operations  15.2 us (3%)
  other arithmetic  14.4 us (3%)
    psum x1, waiting for transfers between devices, single_factors(): right_total = lax.psum(local_right(left_rows, merged), ('gx', 'gy'))  248 us
    psum x2, waiting for transfers between devices, answer_chains(): return psum(psum(frame_in, which_axis), link_axis)  215 us
    dot_general x1, matrix products, on_device(): jnp.einsum('bki,bkj->bij', left_rows, right_rows, precision=HIGHEST)  10.7 us
  transfers between devices with their start and end apart: 3, of which 3 were waited for; matrix products, arithmetic and copies ran while one was open for 0% of the time, Pallas kernels for 0%

profile of v1, /device:TPU:2, one launch (start us, length us, event | category | flops | bytes accessed | tf_op | source)
XLA Modules:
  0.0 535.2 jit_solution(12552644678493231196)
XLA Ops:
  7.2 0.0 copy-start
  7.2 0.0 copy-start.8
  7.2 0.0 all-reduce.11.cloned.1.call-start
  7.2 1.3 copy-done
  8.5 0.0 copy-start.7
  8.5 4.0 convert_add_fusion.1
  12.5 0.0 copy-done.8
  12.5 0.0 copy-done.7
  12.5 0.0 copy-start.1
  12.5 0.0 copy-start.6
  12.5 1.8 convert_add_fusion
  14.4 0.1 copy-done.1
  14.5 0.0 copy-done.6
  14.5 0.0 copy-start.2
  14.5 4.6 convolution_bitcast_fusion.3
  19.1 0.0 copy-done.2
  19.1 4.6 convolution_bitcast_fusion.2
  23.6 0.0 all-reduce.11.cloned.1.call-update
  23.7 0.0 all-reduce.9.cloned.1.call-start
  23.7 65.9 %all-reduce.11.cloned.1.call-done = (f32[1,32,1024]{2,1,0:T(8,128)}, f32[1,32,1024]{2,1,0:T(8,128)}) async-done(((f32[1,32,1024]{2,1,0:T(8,128)}, f32[1,32,1024]{2,1,0:T(8,128)}), (f32[1,32,1024]{2,1,0:T(8,128)}, f32[1,32,1024]{2,1,0:T(8,128)})) %all-reduce.11.cloned.1.call-update) | async-done | bytes 262160 | tf_op jit(solution)/shard_map/psum | solution.py:13
  89.6 0.0 all-reduce.9.cloned.1.call-update
  89.7 0.2 all-reduce.7.cloned.1.call-start
  89.9 149.3 %all-reduce.9.cloned.1.call-done = (f32[1,32,1024]{2,1,0:T(8,128)}, f32[1,32,1024]{2,1,0:T(8,128)}) async-done(((f32[1,32,1024]{2,1,0:T(8,128)}, f32[1,32,1024]{2,1,0:T(8,128)}), (f32[1,32,1024]{2,1,0:T(8,128)}, f32[1,32,1024]{2,1,0:T(8,128)})) %all-reduce.9.cloned.1.call-update) | async-done | bytes 262160 | tf_op jit(solution)/shard_map/psum | solution.py:13
  239.2 1.8 select_reduce_fusion.2
  241.7 0.1 copy.13
  241.8 2.9 custom-call.10
  244.7 0.6 compare_reduce_fusion
  245.3 0.7 fusion.14
  246.0 2.4 custom-call.11
  248.4 1.2 fusion.1
  249.7 1.8 select_reduce_fusion.3
  252.2 0.1 copy.10
  252.3 2.9 custom-call.8
  255.2 0.6 compare_reduce_fusion.1
  255.9 0.7 fusion.13
  256.5 2.4 custom-call.9
  259.0 0.0 copy-start.3
  259.0 1.4 fusion.6
  260.4 5.3 convolution_bitcast_fusion.1
  265.7 0.0 copy-done.3
  265.7 3.1 convolution_bitcast_fusion
  268.9 0.0 all-reduce.7.cloned.1.call-update
  268.9 0.0 copy-start.4
  268.9 248.0 %all-reduce.7.cloned.1.call-done = (f32[1,32,1024]{2,1,0:T(8,128)}, f32[1,32,1024]{2,1,0:T(8,128)}) async-done(((f32[1,32,1024]{2,1,0:T(8,128)}, f32[1,32,1024]{2,1,0:T(8,128)}), (f32[1,32,1024]{2,1,0:T(8,128)}, f32[1,32,1024]{2,1,0:T(8,128)})) %all-reduce.7.cloned.1.call-update) | async-done | bytes 262160 | tf_op jit(solution)/shard_map/psum | solution.py:43
  516.9 1.0 broadcast_multiply_fusion
  517.9 0.0 copy-start.5
  517.9 10.7 %fusion = bf16[2,1024,1024]{2,1,0:T(8,128)(2,1)} fusion(f32[1,1024,1024]{2,1,0:T(8,128)} %bitcast.81, f32[1,1024,1024]{2,1,0:T(8,128)} %bitcast.80, f32[2,32,1024]{2,1,0:T(8,128)S(1)} %pad_maximum_fusion, f32[2,32,1024]{2,1,0:T(8,128)S(1)} %pad_maximum_fusion.1), kind=kOutput, calls=%fused_computation.1 | convolution fusion | flops 811597824 | bytes 13107200 | tf_op jit(solution)/shard_map/bki,bkj->bij/dot_general | solution.py:58
  528.6 0.0 copy-done.4
  528.6 0.0 copy-done.5
  (8 shorter events, 0.1 us)
Async XLA Ops:
  7.2 1.3 copy-start
  7.2 5.3 copy-start.8
  7.2 82.5 %all-reduce.11.cloned.1.call-start = ((), (), s32[]{:S(2)}) async-start(), calls=%async_computation.2 | async-start | bytes 524288 | tf_op jit(solution)/shard_map/psum | solution.py:13
  8.5 4.0 copy-start.7
  12.5 2.0 copy-start.1
  12.5 2.0 copy-start.6
  14.5 4.6 copy-start.2
  23.7 215.5 %all-reduce.9.cloned.1.call-start = ((), (), s32[]{:S(2)}) async-start(), calls=%async_computation.1 | async-start | bytes 524288 | tf_op jit(solution)/shard_map/psum | solution.py:13
  89.7 427.2 %all-reduce.7.cloned.1.call-start = ((), (), s32[]{:S(2)}) async-start(), calls=%async_computation | async-start | bytes 524288 | tf_op jit(solution)/shard_map/psum | solution.py:43
  259.0 6.7 %copy-start.3 = (f32[1024,1024]{1,0:T(8,128)S(1)}, f32[1024,1024]{1,0:T(8,128)}, u32[]{:S(2)}) copy-start(f32[1024,1024]{1,0:T(8,128)} %copy-done.2) | copy-start | bytes 12582916
  268.9 259.7 %copy-start.4 = (f32[2,32,1024]{2,1,0:T(8,128)}, f32[2,32,1024]{2,1,0:T(8,128)S(1)}, u32[]{:S(2)}) copy-start(f32[2,32,1024]{2,1,0:T(8,128)S(1)} %pad_maximum_fusion) | copy-start | bytes 786436
  517.9 10.7 %copy-start.5 = (f32[2,32,1024]{2,1,0:T(8,128)}, f32[2,32,1024]{2,1,0:T(8,128)S(1)}, u32[]{:S(2)}) copy-start(f32[2,32,1024]{2,1,0:T(8,128)S(1)} %pad_maximum_fusion.1) | copy-start | bytes 786436
Sparse Core Ops, SparseCore 0:
  23.8 65.8 all-reduce.10
  93.6 145.5 all-reduce.8
  269.0 247.8 all-reduce.6
